TPU v7x, 512 devices: a whole 4x4x16 slice. The times are simulated.
512 devices in a mesh: seq: 8 (over y, core), expert: 64 (over z, x).
Axes of the slice: x: 4, y: 4, z: 16, core: 2. Of those that a mesh axis runs over, the one named last changes fastest.
Arguments:
- tokens: bfloat16 [65536, 2048], P(('seq', 'expert')), may hold values from -4 to 4
- routes: int32 [65536, 8], P(('seq', 'expert')), may hold values from 0 to 127, all different within a row; in each aligned block of 128 rows (0 to 127, 128 to 255, ...) at most 16 rows name the same one
- gate_shares: int32 [65536, 8], P(('seq', 'expert')), may hold values from 1 to 65536
- gate_up: bfloat16 [128, 2048, 768], P('expert', 'seq'), may hold values from -0.125 to 0.125
Outputs:
- gram: float32 [128, 384, 384], P('expert', 'seq')
- maxima: float32 [128, 2048], P('expert', 'seq')
Inputs may be any that keep to these rules, and one draw needn't show every extreme that they name: `routes`: among the 128 rows of one device no expert is named more than 16 times.
All inputs are finite; a program needn't handle non-finite values.
Results may differ from a plain program's by a relative error of at most 0.0049.
Values may be sent and summed in bfloat16 or wider, within the bound.
A program may use at most 64 MiB of HBM per device.

v0:
```python
import jax
import jax.numpy as jnp
from jax import lax
from jax.sharding import PartitionSpec as P

D = 2048
FWIN = 384


def hidden_of(projected):
    return (jax.nn.silu(projected[..., :FWIN]) * projected[..., FWIN:]).astype(jnp.bfloat16)


def split_weighted(hidden, row_shares):
    weighted = hidden.astype(jnp.float32) * row_shares[..., None]
    weighted_high = weighted.astype(jnp.bfloat16)
    weighted_low = (weighted - weighted_high.astype(jnp.float32)).astype(jnp.bfloat16)
    return (weighted_high, weighted_low)


def body(tokens, routes, gate_shares, gate_up):
    tok_rows = tokens.shape[0]
    top_count = routes.shape[1]
    expert_count = lax.axis_size("expert")
    seq_count = lax.axis_size("seq")
    local_count = gate_up.shape[0]
    all_experts = local_count * expert_count
    capacity = 2 * tok_rows * top_count // all_experts
    norm_factor = all_experts / (tok_rows * seq_count * expert_count * top_count)
    chosen = routes.reshape(-1)
    shares = gate_shares.reshape(-1).astype(jnp.float32) / 65536.0
    one_hot = (chosen[:, None] == jnp.arange(all_experts, dtype=jnp.int32)[None, :]).astype(
        jnp.int32
    )
    ranked = jnp.sum((jnp.cumsum(one_hot, axis=0) - one_hot) * one_hot, axis=1)
    slot_index = chosen * capacity + ranked
    token_index = jnp.arange(tok_rows * top_count, dtype=jnp.int32) // top_count
    outgoing_rows = (
        jnp.zeros((all_experts * capacity, D), jnp.bfloat16).at[slot_index].set(tokens[token_index])
    )
    out_shares = jnp.zeros((all_experts * capacity,), jnp.float32).at[slot_index].set(shares)
    outgoing_rows = outgoing_rows.reshape(expert_count, local_count, capacity, D)
    out_shares = out_shares.reshape(expert_count, local_count, capacity)
    arrived, arrived_shares = (
        lax.all_to_all(outgoing_rows, "expert", split_axis=0, concat_axis=0, tiled=True),
        lax.all_to_all(
            out_shares.astype(jnp.bfloat16), "expert", split_axis=0, concat_axis=0, tiled=True
        ).astype(out_shares.dtype),
    )
    is_live = arrived_shares > 0.0
    channel_max = jnp.max(jnp.where(is_live[..., None], jnp.abs(arrived), 0), axis=(0, 2)).astype(
        jnp.float32
    )
    projected = jnp.einsum(
        "slcd,ldf->lscf",
        arrived,
        lax.all_gather(gate_up, "seq", axis=1, tiled=True),
        preferred_element_type=jnp.float32,
    )
    hidden = hidden_of(projected).reshape(local_count, expert_count * capacity, FWIN)
    row_shares = jnp.transpose(arrived_shares, (1, 0, 2)).reshape(
        local_count, expert_count * capacity
    )
    weighted_high, weighted_low = split_weighted(hidden, row_shares)
    gram_part = jnp.einsum(
        "lrf,lrg->lfg", hidden, weighted_high, preferred_element_type=jnp.float32
    )
    gram_part = gram_part + jnp.einsum(
        "lrf,lrg->lfg", hidden, weighted_low, preferred_element_type=jnp.float32
    )
    gram_part = gram_part * norm_factor
    gram = lax.psum_scatter(gram_part, "seq", scatter_dimension=1, tiled=True)
    full_max = lax.pmax(channel_max, "seq")
    slice_width = D // seq_count
    maxima = lax.dynamic_slice_in_dim(full_max, lax.axis_index("seq") * slice_width, slice_width, 1)
    return (gram, maxima)


def solution(mesh):
    return jax.shard_map(
        body,
        mesh=mesh,
        in_specs=(
            P(("seq", "expert"), None),
            P(("seq", "expert"), None),
            P(("seq", "expert"), None),
            P("expert", "seq", None),
        ),
        out_specs=(P("expert", "seq", None), P("expert", "seq")),
        check_vma=False,
    )
```

profile of v0, /device:TPU:2, one launch (start us, length us, event | category | flops | bytes accessed | tf_op | source)
XLA Modules:
  0.0 496.8 jit_solution(5624225172314754121)
XLA Ops:
  7.2 0.0 copy-start
  7.2 0.0 copy-start.1
  7.2 0.8 copy.20
  8.0 0.1 eq.29
  8.1 0.1 eq.25
  8.2 0.7 broadcast_multiply_fusion
  8.9 0.1 copy.22
  9.0 0.2 fusion.21
  9.3 0.1 copy.23
  9.4 0.1 copy.19
  9.5 0.1 mul.47
  9.6 0.0 copy-done.1
  9.6 0.1 copy.25
  9.7 0.1 reshape.130
  9.8 0.4 fusion.20
  10.2 4.3 scatter_custom_fusion.1
  14.6 0.7 convert_element_type.46
  15.3 18.6 %all-to-all-start.1 = ((bf16[64,2,16]{2,1,0:T(2,128)(2,1)}), bf16[64,2,16]{2,1,0:T(2,128)(2,1)S(1)}, u32[]{:S(2)}, u32[]{:S(2)}) async-start(bf16[64,2,16]{2,1,0:T(2,128)(2,1)} %convert_element_type.46), calls=%async_computation.1 | async-start | bytes 65536 | tf_op jit(solution)/shard_map/all_to_all | solution.py:46
  33.9 0.0 copy-done
  34.0 24.9 %scatter_custom_fusion = bf16[2048,2048]{1,0:T(8,128)(2,1)} fusion(s32[1024]{0:T(1024)S(1)} %bitcast.30, bf16[128,2048]{1,0:T(8,128)(2,1)S(1)} %copy-done, s32[1024]{0:T(1024)S(1)} %broadcast_clamp_fusion, bf16[]{:T(256)} %constant.19.clone.1), kind=kCustom, calls=%fused_computation.7 | custom fusion | bytes 8388610 | tf_op jit(solution)/shard_map/scatter | solution.py:39
  58.9 0.0 all-to-all-done.1
  58.9 15.3 %all-to-all-start = ((bf16[64,2,16,2048]{3,2,1,0:T(8,128)(2,1)}), bf16[64,2,16,2048]{3,2,1,0:T(8,128)(2,1)}, u32[]{:S(2)}, u32[]{:S(2)}) async-start(bf16[64,2,16,2048]{3,2,1,0:T(8,128)(2,1)} %bitcast.24), calls=%async_computation | async-start | bytes 16777216 | tf_op jit(solution)/shard_map/all_to_all | solution.py:45
  74.2 0.0 all-gather.2.cloned.1.call-start
  74.2 0.7 all-gather.2.cloned.1.call-update
  74.9 0.0 reduce-scatter.2.cloned.1.call-start
  75.0 0.1 mul.51
  75.1 51.5 %all-gather.2.cloned.1.call-done = bf16[2,2048,768]{2,1,0:T(8,128)(2,1)} async-done(((bf16[2,256,768]{2,1,0:T(8,128)(2,1)}), bf16[2,2048,768]{2,1,0:T(8,128)(2,1)}) %all-gather.2.cloned.1.call-update) | async-done | bytes 6291472 | tf_op jit(solution)/shard_map/all_gather | solution.py:57
  126.6 316.8 %all-to-all-done = bf16[64,2,16,2048]{3,2,1,0:T(8,128)(2,1)} async-done(((bf16[64,2,16,2048]{3,2,1,0:T(8,128)(2,1)}), bf16[64,2,16,2048]{3,2,1,0:T(8,128)(2,1)}, u32[]{:S(2)}, u32[]{:S(2)}) %all-to-all-start) | async-done | bytes 8388640 | tf_op jit(solution)/shard_map/all_to_all | solution.py:45
  443.3 10.0 %fusion = f32[2,64,16,768]{3,2,1,0:T(8,128)S(1)} fusion(bf16[64,2,16,2048]{3,2,1,0:T(8,128)(2,1)} %all-to-all-done, bf16[2,2048,768]{2,1,0:T(8,128)(2,1)} %all-gather.2.cloned.1.call-done), kind=kOutput, calls=%fused_computation.3 | convolution fusion | flops 6442450944 | bytes 20971520 | tf_op jit(solution)/shard_map/slcd,ldf->lscf/dot_general | solution.py:54
  453.4 0.9 fusion.6
  454.3 1.2 fusion.10
  455.5 2.3 fusion.16
  457.9 0.0 reduce-scatter.2.cloned.1.call-update
  458.0 5.2 %select_reduce_fusion = bf16[2,2048]{1,0:T(2,128)(2,1)S(1)} fusion(bf16[64,2,16,2048]{3,2,1,0:T(8,128)(2,1)} %all-to-all-done, pred[64,2,16]{2,1,0:T(4,128)(4,1)S(1)} %convert_compare_fusion), kind=kLoop, calls=%fused_computation.5 | loop fusion | flops 12578816 | bytes 8398848 | tf_op jit(solution)/shard_map/reduce_max | solution.py:51
  463.1 23.7 %pmax.7 = f32[2,2048]{1,0:T(2,128)S(1)} all-reduce(bf16[2,2048]{1,0:T(2,128)(2,1)S(1)} %select_reduce_fusion), channel_id=1, replica_groups=mesh['seq'=8,'expert'=64] {'seq'}, use_global_device_ids=true, to_apply=%region_7.8 | all-reduce | flops 4096 | bytes 24576 | tf_op jit(solution)/shard_map/pmax | solution.py:73
  486.8 0.6 constant_dynamic-slice_fusion
  487.4 2.5 reduce-scatter.2.cloned.1.call-done
  (12 shorter events, 0.2 us)
Async XLA Ops:
  7.2 26.8 %copy-start = (bf16[128,2048]{1,0:T(8,128)(2,1)S(1)}, bf16[128,2048]{1,0:T(8,128)(2,1)}, u32[]{:S(2)}) copy-start(bf16[128,2048]{1,0:T(8,128)(2,1)} %param.4) | copy-start | bytes 1572868
  7.2 2.4 copy-start.1
  15.3 43.6 %all-to-all-start.1 = ((bf16[64,2,16]{2,1,0:T(2,128)(2,1)}), bf16[64,2,16]{2,1,0:T(2,128)(2,1)S(1)}, u32[]{:S(2)}, u32[]{:S(2)}) async-start(bf16[64,2,16]{2,1,0:T(2,128)(2,1)} %convert_element_type.46), calls=%async_computation.1 | async-start | bytes 65536 | tf_op jit(solution)/shard_map/all_to_all | solution.py:46
  58.9 384.4 %all-to-all-start = ((bf16[64,2,16,2048]{3,2,1,0:T(8,128)(2,1)}), bf16[64,2,16,2048]{3,2,1,0:T(8,128)(2,1)}, u32[]{:S(2)}, u32[]{:S(2)}) async-start(bf16[64,2,16,2048]{3,2,1,0:T(8,128)(2,1)} %bitcast.24), calls=%async_computation | async-start | bytes 16777216 | tf_op jit(solution)/shard_map/all_to_all | solution.py:45
  74.2 52.4 %all-gather.2.cloned.1.call-start = ((), (), s32[]{:S(2)}) async-start(), calls=%async_computation.3 | async-start | bytes 7077888 | tf_op jit(solution)/shard_map/all_gather | solution.py:57
  74.9 415.0 %reduce-scatter.2.cloned.1.call-start = ((), (), s32[]{:S(2)}) async-start(), calls=%async_computation.4 | async-start | bytes 1327104 | tf_op jit(solution)/shard_map/reduce_scatter | solution.py:72
Sparse Core Ops, SparseCore 0:
  77.1 49.4 all-gather.1
  458.0 31.8 reduce-scatter.1
where the time goes:
time: 497 us
  waiting for transfers between devices  371 us (75%)
  starting transfers between devices  34 us (7%)
  local copies, waits for them, and re-layouts  32.3 us (6%)
  blocking collectives  23.7 us (5%)
  between operations  14.2 us (3%)
  matrix products  13.6 us (3%)
  other arithmetic  7.54 us (2%)
    all_to_all x1, waiting for transfers between devices, body(): lax.all_to_all(outgoing_rows, 'expert', split_axis=0, concat_axis=0, tile...  317 us
    all_gather x1, waiting for transfers between devices, body(): lax.all_gather(gate_up, 'seq', axis=1, tiled=True)  51.5 us
    scatter x1, local copies, waits for them, and re-layouts, body(): jnp.zeros((all_experts * capacity, D), jnp.bfloat16).at[slot_index]  24.9 us
    pmax x1, blocking collectives, body(): full_max = lax.pmax(channel_max, 'seq')  23.7 us
    all_to_all x1, starting transfers between devices, body(): lax.all_to_all(out_shares.astype(jnp.bfloat16), 'expert', split_axis=0, c...  18.6 us
    all_to_all x1, starting transfers between devices, body(): lax.all_to_all(outgoing_rows, 'expert', split_axis=0, concat_axis=0, tile...  15.3 us
    dot_general x1, matrix products, body(): jnp.einsum('slcd,ldf->lscf', arrived, lax.all_gather(gate_up, 'seq', axis...  10 us
  transfers between devices with their start and end apart: 4, of which 3 were waited for; matrix products, arithmetic and copies ran while one was open for 6% of the time, Pallas kernels for 0%

commit v1 on v0

--- a/solution.py
+++ b/solution.py
@@ -5,6 +5,27 @@
 
 D = 2048
 FWIN = 384
+
+
+def gather_around(value, axis, dim):
+    size, here, span = (lax.axis_size(axis), lax.axis_index(axis), value.shape[dim])
+    right = [(i, (i + 1) % size) for i in range(size)]
+    behind = [(i, (i - 1) % size) for i in range(size)]
+    filled = jnp.zeros((*value.shape[:dim], size * span, *value.shape[dim + 1 :]), value.dtype)
+    filled = lax.dynamic_update_slice_in_dim(filled, value, here * span, axis=dim)
+    from_left = from_right = value
+    half = size // 2
+    for turn in range(1, half + 1):
+        from_left = lax.ppermute(from_left, axis, right)
+        filled = lax.dynamic_update_slice_in_dim(
+            filled, from_left, (here - turn) % size * span, axis=dim
+        )
+        if turn < size - half:
+            from_right = lax.ppermute(from_right, axis, behind)
+            filled = lax.dynamic_update_slice_in_dim(
+                filled, from_right, (here + turn) % size * span, axis=dim
+            )
+    return filled
 
 
 def hidden_of(projected):
@@ -54,7 +75,7 @@
     projected = jnp.einsum(
         "slcd,ldf->lscf",
         arrived,
-        lax.all_gather(gate_up, "seq", axis=1, tiled=True),
+        gather_around(gate_up, "seq", 1),
         preferred_element_type=jnp.float32,
     )
     hidden = hidden_of(projected).reshape(local_count, expert_count * capacity, FWIN)

time: 497 us -> 498 us (level)
  waiting for transfers between devices: 371 us -> 348 us
  local copies, waits for them, and re-layouts: 32.3 us -> 46.3 us
  starting transfers between devices: 34 us -> 43.4 us
    all_gather x1 -> x0, waiting for transfers between devices: 51.5 us -> none  [body(): lax.all_gather(gate_up, 'seq', axis=1, tiled=True)]
    ppermute x0 -> x7, waiting for transfers between devices: none -> 28.6 us  [the longest x4 28.6 us: gather_around(): from_left = lax.ppermute(from_left, axis, right)]
    dynamic_update_slice x0 -> x8, local copies, waits for them, and re-layouts: none -> 11 us  [the longest x4 6.09 us: gather_around(): lax.dynamic_update_slice_in_dim(filled, from_left, (here - turn) % size *...]
    ppermute x0 -> x7, starting transfers between devices: none -> 9.3 us  [the longest x3 9.28 us: gather_around(): from_right = lax.ppermute(from_right, axis, behind)]
  transfers between devices with their start and end apart: 4 -> 10, of which waited for: 3 -> 6; matrix products, arithmetic and copies ran while one was open for 6% -> 9% of each run, Pallas kernels for 0% -> 0%
where the time goes in v1:
time: 498 us
  waiting for transfers between devices  348 us (70%)
  local copies, waits for them, and re-layouts  46.3 us (9%)
  starting transfers between devices  43.4 us (9%)
  blocking collectives  23.7 us (5%)
  between operations  14.2 us (3%)
  matrix products  13.6 us (3%)
  other arithmetic  8.27 us (2%)
    all_to_all x1, waiting for transfers between devices, body(): lax.all_to_all(outgoing_rows, 'expert', split_axis=0, concat_axis=0, tile...  317 us
    ppermute x4, waiting for transfers between devices, gather_around(): from_left = lax.ppermute(from_left, axis, right)  28.6 us
    scatter x1, local copies, waits for them, and re-layouts, body(): jnp.zeros((all_experts * capacity, D), jnp.bfloat16).at[slot_index]  24.9 us
    pmax x1, blocking collectives, body(): full_max = lax.pmax(channel_max, 'seq')  23.7 us
    all_to_all x1, starting transfers between devices, body(): lax.all_to_all(out_shares.astype(jnp.bfloat16), 'expert', split_axis=0, c...  18.6 us
    all_to_all x1, starting transfers between devices, body(): lax.all_to_all(outgoing_rows, 'expert', split_axis=0, concat_axis=0, tile...  15.4 us
    dot_general x1, matrix products, body(): jnp.einsum('slcd,ldf->lscf', arrived, gather_around(gate_up, 'seq', 1), p...  10 us
  transfers between devices with their start and end apart: 10, of which 6 were waited for; matrix products, arithmetic and copies ran while one was open for 9% of the time, Pallas kernels for 0%

profile of v1, /device:TPU:2, one launch (start us, length us, event | category | flops | bytes accessed | tf_op | source)
XLA Modules:
  0.0 497.6 jit_solution(5991794042135191551)
XLA Ops:
  7.2 0.0 copy-start
  7.2 0.7 broadcast_multiply_fusion
  7.9 0.8 copy.20
  8.7 0.1 eq.37
  8.8 0.1 eq.33
  8.9 0.1 copy.19
  9.0 0.1 mul.69
  9.1 0.1 copy.22
  9.2 0.2 fusion.21
  9.5 0.1 copy.23
  9.6 0.7 convert_multiply_fusion.1
  10.3 0.1 copy.25
  10.4 0.1 reshape.130
  10.5 0.4 fusion.20
  10.9 4.3 scatter_custom_fusion.1
  15.2 0.7 convert_element_type.46
  15.9 18.6 %all-to-all-start.1 = ((bf16[64,2,16]{2,1,0:T(2,128)(2,1)}), bf16[64,2,16]{2,1,0:T(2,128)(2,1)S(1)}, u32[]{:S(2)}, u32[]{:S(2)}) async-start(bf16[64,2,16]{2,1,0:T(2,128)(2,1)} %convert_element_type.46), calls=%async_computation.1 | async-start | bytes 65536 | tf_op jit(solution)/shard_map/all_to_all | solution.py:67
  34.6 0.0 copy-done
  34.6 24.9 %scatter_custom_fusion = bf16[2048,2048]{1,0:T(8,128)(2,1)} fusion(s32[1024]{0:T(1024)S(1)} %bitcast.30, bf16[128,2048]{1,0:T(8,128)(2,1)S(1)} %copy-done, s32[1024]{0:T(1024)S(1)} %broadcast_clamp_fusion, bf16[]{:T(256)} %constant.80.clone.1), kind=kCustom, calls=%fused_computation.7 | custom fusion | bytes 8388610 | tf_op jit(solution)/shard_map/scatter | solution.py:60
  59.5 0.0 all-to-all-done.1
  59.5 0.0 copy-start.1
  59.5 15.4 %all-to-all-start = ((bf16[64,2,16,2048]{3,2,1,0:T(8,128)(2,1)}), bf16[64,2,16,2048]{3,2,1,0:T(8,128)(2,1)}, u32[]{:S(2)}, u32[]{:S(2)}) async-start(bf16[64,2,16,2048]{3,2,1,0:T(8,128)(2,1)} %bitcast.24), calls=%async_computation | async-start | bytes 16777216 | tf_op jit(solution)/shard_map/all_to_all | solution.py:66
  75.0 0.0 reduce-scatter.2.cloned.1.call-start
  75.0 0.0 copy-done.1
  75.0 0.0 collective-permute-start
  75.0 2.9 collective-permute-start.1
  78.0 9.7 %collective-permute-done = bf16[2,256,768]{2,1,0:T(8,128)(2,1)S(1)} collective-permute-done((bf16[2,256,768]{2,1,0:T(8,128)(2,1)S(1)}, bf16[2,256,768]{2,1,0:T(8,128)(2,1)S(1)}, u32[]{:S(2)}, u32[]{:S(2)}) %collective-permute-start) | collective-permute-done | bytes 786464 | tf_op jit(solution)/shard_map/ppermute | solution.py:19
  87.7 0.0 collective-permute-start.2
  87.7 0.0 collective-permute-done.1
  87.7 3.4 collective-permute-start.3
  91.0 9.4 %collective-permute-done.2 = bf16[2,256,768]{2,1,0:T(8,128)(2,1)} collective-permute-done((bf16[2,256,768]{2,1,0:T(8,128)(2,1)S(1)}, bf16[2,256,768]{2,1,0:T(8,128)(2,1)}, u32[]{:S(2)}, u32[]{:S(2)}) %collective-permute-start.2) | collective-permute-done | bytes 786464 | tf_op jit(solution)/shard_map/ppermute | solution.py:19
  100.4 0.0 collective-permute-start.4
  100.4 3.1 broadcast_in_dim.27
  103.5 0.9 constant_dynamic-update-slice_fusion.7
  104.4 0.0 collective-permute-done.3
  104.4 3.0 collective-permute-start.5
  107.4 0.1 mul.81
  107.5 5.8 %collective-permute-done.4 = bf16[2,256,768]{2,1,0:T(8,128)(2,1)} collective-permute-done((bf16[2,256,768]{2,1,0:T(8,128)(2,1)}, bf16[2,256,768]{2,1,0:T(8,128)(2,1)}, u32[]{:S(2)}, u32[]{:S(2)}) %collective-permute-start.4) | collective-permute-done | bytes 786464 | tf_op jit(solution)/shard_map/ppermute | solution.py:19
  113.3 0.0 collective-permute-start.6
  113.3 1.0 constant_dynamic-update-slice_fusion.6
  114.3 0.9 constant_dynamic-update-slice_fusion.5
  115.2 2.1 constant_dynamic-update-slice_fusion.4
  117.3 2.0 constant_dynamic-update-slice_fusion.3
  119.4 2.1 constant_dynamic-update-slice_fusion.2
  121.4 0.0 collective-permute-done.5
  121.4 1.0 constant_dynamic-update-slice_fusion.1
  122.4 3.8 collective-permute-done.6
  126.2 1.0 constant_dynamic-update-slice_fusion
  127.2 317.0 %all-to-all-done = bf16[64,2,16,2048]{3,2,1,0:T(8,128)(2,1)} async-done(((bf16[64,2,16,2048]{3,2,1,0:T(8,128)(2,1)}), bf16[64,2,16,2048]{3,2,1,0:T(8,128)(2,1)}, u32[]{:S(2)}, u32[]{:S(2)}) %all-to-all-start) | async-done | bytes 8388640 | tf_op jit(solution)/shard_map/all_to_all | solution.py:66
  444.1 10.0 %fusion = f32[2,64,16,768]{3,2,1,0:T(8,128)S(1)} fusion(bf16[64,2,16,2048]{3,2,1,0:T(8,128)(2,1)} %all-to-all-done, bf16[2,2048,768]{2,1,0:T(8,128)(2,1)} %constant_dynamic-update-slice_fusion), kind=kOutput, calls=%fused_computation.3 | convolution fusion | flops 6442450944 | bytes 20971520 | tf_op jit(solution)/shard_map/slcd,ldf->lscf/dot_general | solution.py:75
  454.2 0.9 fusion.6
  455.1 1.2 fusion.10
  456.3 2.3 fusion.16
  458.7 0.0 reduce-scatter.2.cloned.1.call-update
  458.7 5.2 %select_reduce_fusion = bf16[2,2048]{1,0:T(2,128)(2,1)S(1)} fusion(bf16[64,2,16,2048]{3,2,1,0:T(8,128)(2,1)} %all-to-all-done, pred[64,2,16]{2,1,0:T(4,128)(4,1)S(1)} %convert_compare_fusion), kind=kLoop, calls=%fused_computation.5 | loop fusion | flops 12578816 | bytes 8398848 | tf_op jit(solution)/shard_map/reduce_max | solution.py:72
  463.9 23.7 %pmax.7 = f32[2,2048]{1,0:T(2,128)S(1)} all-reduce(bf16[2,2048]{1,0:T(2,128)(2,1)S(1)} %select_reduce_fusion), channel_id=1, replica_groups=mesh['seq'=8,'expert'=64] {'seq'}, use_global_device_ids=true, to_apply=%region_7.8 | all-reduce | flops 4096 | bytes 24576 | tf_op jit(solution)/shard_map/pmax | solution.py:94
  487.6 0.6 constant_dynamic-slice_fusion
  488.2 2.5 reduce-scatter.2.cloned.1.call-done
  (10 shorter events, 0.2 us)
Async XLA Ops:
  7.2 27.4 %copy-start = (bf16[128,2048]{1,0:T(8,128)(2,1)S(1)}, bf16[128,2048]{1,0:T(8,128)(2,1)}, u32[]{:S(2)}) copy-start(bf16[128,2048]{1,0:T(8,128)(2,1)} %param.4) | copy-start | bytes 1572868
  15.9 43.6 %all-to-all-start.1 = ((bf16[64,2,16]{2,1,0:T(2,128)(2,1)}), bf16[64,2,16]{2,1,0:T(2,128)(2,1)S(1)}, u32[]{:S(2)}, u32[]{:S(2)}) async-start(bf16[64,2,16]{2,1,0:T(2,128)(2,1)} %convert_element_type.46), calls=%async_computation.1 | async-start | bytes 65536 | tf_op jit(solution)/shard_map/all_to_all | solution.py:67
  59.5 15.5 %copy-start.1 = (bf16[2,256,768]{2,1,0:T(8,128)(2,1)S(1)}, bf16[2,256,768]{2,1,0:T(8,128)(2,1)}, u32[]{:S(2)}) copy-start(bf16[2,256,768]{2,1,0:T(8,128)(2,1)} %param.7) | copy-start | bytes 2359300
  59.5 384.6 %all-to-all-start = ((bf16[64,2,16,2048]{3,2,1,0:T(8,128)(2,1)}), bf16[64,2,16,2048]{3,2,1,0:T(8,128)(2,1)}, u32[]{:S(2)}, u32[]{:S(2)}) async-start(bf16[64,2,16,2048]{3,2,1,0:T(8,128)(2,1)} %bitcast.24), calls=%async_computation | async-start | bytes 16777216 | tf_op jit(solution)/shard_map/all_to_all | solution.py:66
  75.0 415.8 %reduce-scatter.2.cloned.1.call-start = ((), (), s32[]{:S(2)}) async-start(), calls=%async_computation.3 | async-start | bytes 1327104 | tf_op jit(solution)/shard_map/reduce_scatter | solution.py:93
  75.0 12.6 %collective-permute-start = (bf16[2,256,768]{2,1,0:T(8,128)(2,1)S(1)}, bf16[2,256,768]{2,1,0:T(8,128)(2,1)S(1)}, u32[]{:S(2)}, u32[]{:S(2)}) collective-permute-start(bf16[2,256,768]{2,1,0:T(8,128)(2,1)S(1)} %copy-done.1), channel_id=1, source_target_pairs={{0,64},{64,128},{128,192},{192,256},{256,320},{320,384},{384,448},... | collective-permute-start | bytes 2359304 | tf_op jit(solution)/shard_map/ppermute | solution.py:19
  75.0 12.6 %collective-permute-start.1 = (bf16[2,256,768]{2,1,0:T(8,128)(2,1)S(1)}, bf16[2,256,768]{2,1,0:T(8,128)(2,1)S(1)}, u32[]{:S(2)}, u32[]{:S(2)}) collective-permute-start(bf16[2,256,768]{2,1,0:T(8,128)(2,1)S(1)} %copy-done.1), channel_id=1, source_target_pairs={{0,448},{64,0},{128,64},{192,128},{256,192},{320,256},{384,320},{4... | collective-permute-start | bytes 2359304 | tf_op jit(solution)/shard_map/ppermute | solution.py:24
  87.7 12.7 %collective-permute-start.2 = (bf16[2,256,768]{2,1,0:T(8,128)(2,1)S(1)}, bf16[2,256,768]{2,1,0:T(8,128)(2,1)}, u32[]{:S(2)}, u32[]{:S(2)}) collective-permute-start(bf16[2,256,768]{2,1,0:T(8,128)(2,1)S(1)} %collective-permute-done), channel_id=1, source_target_pairs={{0,64},{64,128},{128,192},{192,256},{256,320},{320,384},{384,448},... | collective-permute-start | bytes 2359304 | tf_op jit(solution)/shard_map/ppermute | solution.py:19
  87.7 16.7 %collective-permute-start.3 = (bf16[2,256,768]{2,1,0:T(8,128)(2,1)S(1)}, bf16[2,256,768]{2,1,0:T(8,128)(2,1)}, u32[]{:S(2)}, u32[]{:S(2)}) collective-permute-start(bf16[2,256,768]{2,1,0:T(8,128)(2,1)S(1)} %collective-permute-done.1), channel_id=1, source_target_pairs={{0,448},{64,0},{128,64},{192,128},{256,192},{320,256},{384,320},{4... | collective-permute-start | bytes 2359304 | tf_op jit(solution)/shard_map/ppermute | solution.py:24
  100.4 12.9 %collective-permute-start.4 = (bf16[2,256,768]{2,1,0:T(8,128)(2,1)}, bf16[2,256,768]{2,1,0:T(8,128)(2,1)}, u32[]{:S(2)}, u32[]{:S(2)}) collective-permute-start(bf16[2,256,768]{2,1,0:T(8,128)(2,1)} %collective-permute-done.2), channel_id=1, source_target_pairs={{0,64},{64,128},{128,192},{192,256},{256,320},{320,384},{384,448},... | collective-permute-start | bytes 2359304 | tf_op jit(solution)/shard_map/ppermute | solution.py:19
  104.4 17.0 %collective-permute-start.5 = (bf16[2,256,768]{2,1,0:T(8,128)(2,1)}, bf16[2,256,768]{2,1,0:T(8,128)(2,1)S(1)}, u32[]{:S(2)}, u32[]{:S(2)}) collective-permute-start(bf16[2,256,768]{2,1,0:T(8,128)(2,1)} %collective-permute-done.3), channel_id=1, source_target_pairs={{0,448},{64,0},{128,64},{192,128},{256,192},{320,256},{384,320},{4... | collective-permute-start | bytes 2359304 | tf_op jit(solution)/shard_map/ppermute | solution.py:24
  113.3 12.8 %collective-permute-start.6 = (bf16[2,256,768]{2,1,0:T(8,128)(2,1)}, bf16[2,256,768]{2,1,0:T(8,128)(2,1)S(1)}, u32[]{:S(2)}, u32[]{:S(2)}) collective-permute-start(bf16[2,256,768]{2,1,0:T(8,128)(2,1)} %collective-permute-done.4), channel_id=1, source_target_pairs={{0,64},{64,128},{128,192},{192,256},{256,320},{320,384},{384,448},... | collective-permute-start | bytes 2359304 | tf_op jit(solution)/shard_map/ppermute | solution.py:19
Sparse Core Ops, SparseCore 0:
  458.8 31.8 reduce-scatter.1
